TPU v7x, 128 devices: a whole 4x4x4 slice. The times are simulated.
128 devices in a mesh: req: 4 (over y), seq: 32 (over x, z, core).
Axes of the slice: x: 4, y: 4, z: 4, core: 2. Of those that a mesh axis runs over, the one named last changes fastest.
Arguments:
- tokens: bfloat16 [4, 4096, 2048], P('req', 'seq'), may hold values from -6 to 6
- lengths: int32 [4, 4], replicated, may hold values from 1 to 2048, as said below
- attn_gain: bfloat16 [2048], replicated, may hold values from 0.099609375 to 1.8984375
- w_query: bfloat16 [2048, 512], replicated, may hold values from -0.125 to 0.125
- w_key: bfloat16 [2048, 512], replicated, may hold values from -0.125 to 0.125
- w_value: bfloat16 [2048, 1024], replicated, may hold values from -0.125 to 0.125
- w_outgate: bfloat16 [2048, 1024], replicated, may hold values from -0.125 to 0.125
- gate_down: bfloat16 [2048, 16], replicated, may hold values from -1 to 1
- gate_up: bfloat16 [16, 512], replicated, may hold values from -2 to 2
- gate_bias: float32 [512], replicated, may hold values from -1 to 8
- conv_weight: bfloat16 [4, 2048], replicated, may hold values from -2 to 2
- head_gain: bfloat16 [512], replicated, may hold values from 0.099609375 to 1.8984375
- w_out: bfloat16 [1024, 2048], replicated, may hold values from -0.1875 to 0.1875
- forward_norm_scale: bfloat16 [2048], replicated, may hold values from 0.099609375 to 1.8984375
- w_gate: bfloat16 [2048, 2816], P('seq', 'req'), may hold values from -0.125 to 0.125
- w_up: bfloat16 [2048, 2816], P('seq', 'req'), may hold values from -0.125 to 0.125
- down_weight: bfloat16 [2048, 2816], P('seq', 'req'), may hold values from -0.109375 to 0.109375
Outputs:
- output: bfloat16 [4, 4096, 2048], P('req', 'seq')
Inputs may be any that keep to these rules, and one draw needn't show every extreme that they name: Row g lists the prompt lengths of group g's 4 requests, packed in slot order from position 0 of the group; every row holds one length equal to 2048; rows 2i and 2i + 1 together sum to 6144, so all rows sum to 12288; each row sums to between 2052 and 4092.
All inputs are finite; a program needn't handle non-finite values.
Results may differ from a plain program's by a relative error of at most 0.008.
Values may be sent and summed in bfloat16 or wider, within the bound.
A program may use at most 128 MiB of HBM per device.

v0:
```python
import jax
import jax.numpy as jnp
from jax import lax
from jax.sharding import PartitionSpec as P

HEADS = 2
SPAN = 64
EPSILON = 1e-05
NORMALIZER = 16.0
MAXIMUM_ACCURACY = lax.Precision.HIGHEST


def prefix_2(shard, axis, combine, identity):
    size, mine = (lax.axis_size(axis), lax.axis_index(axis))
    everything = jax.tree.map(lambda part: lax.all_gather(part, axis), shard)
    start = jax.tree.map(
        lambda part, zero: jnp.broadcast_to(jnp.asarray(zero, part.dtype), part.shape),
        shard,
        identity,
    )

    def lap(k, before):
        reached = k < mine
        new = combine(before, jax.tree.map(lambda part: part[k], everything))
        return jax.tree.map(lambda a, b: jnp.where(reached, a, b), new, before)

    return lax.fori_loop(0, size, lap, start)


def from_behind(value, axis, steps):
    count = lax.axis_size(axis)
    initial, last = (max(0, -steps), min(count, count - steps))
    return lax.ppermute(value, axis, [(source, source + steps) for source in range(initial, last)])


def rms_scale(values, gain):
    mean_square = jnp.mean(values * values, axis=-1, keepdims=True)
    return values * lax.rsqrt(mean_square + EPSILON) * gain


def segment_ids(positions, bounds):
    return jnp.sum((positions[:, None] >= bounds[None, :]).astype(jnp.int32), axis=1)


def pick_group(table, indices):
    match = indices[:, None] == jnp.arange(table.shape[0], dtype=jnp.int32)[None, :]
    return jnp.sum(jnp.where(match, table[None, :], 0), axis=1)


def short_conv(extended, segment_ext, conv_weight, count):
    taps = conv_weight.shape[0]
    own_segment = segment_ext[taps - 1 :]
    total = jnp.zeros((count, extended.shape[1]), jnp.float32)
    for tap_index in range(taps):
        first = taps - 1 - tap_index
        shifted = extended[first : first + count].astype(jnp.float32)
        same = (segment_ext[first : first + count] == own_segment).astype(jnp.float32)
        total = total + conv_weight[tap_index].astype(jnp.float32) * shifted * same[:, None]
    return total


def span_cumulative(log_decay):
    span_len, head_count, key_width = log_decay.shape
    lower = jnp.tril(jnp.ones((span_len, span_len), jnp.float32))
    flat = jnp.dot(
        lower, log_decay.reshape(span_len, head_count * key_width), precision=MAXIMUM_ACCURACY
    )
    return flat.reshape(span_len, head_count, key_width)


def state_update(
    recurrent_state, cumulative, keys_float, value_rows_wide, segment_span, clean_last
):
    tail = cumulative[-1]
    keep = (segment_span == segment_span[-1]).astype(jnp.float32)
    weighted_values = keys_float * jnp.exp(tail[None] - cumulative) * keep[:, None, None]
    state_increment = jnp.einsum(
        "ugl,ugi->gli", weighted_values, value_rows_wide, precision=MAXIMUM_ACCURACY
    )
    return recurrent_state * (jnp.exp(tail) * clean_last)[:, :, None] + state_increment


def span_state(recurrent_state, items):
    query, keys, values, log_decay, segment_span, segment_before = items
    cumulative = span_cumulative(log_decay)
    clean_last = (segment_span[-1] == segment_before).astype(jnp.float32)
    new_state = state_update(
        recurrent_state,
        cumulative,
        keys.astype(jnp.float32),
        values.astype(jnp.float32),
        segment_span,
        clean_last,
    )
    return (new_state, None)


def span_attend(recurrent_state, items):
    query, keys, values, log_decay, segment_span, segment_before = items
    cumulative = span_cumulative(log_decay)
    query_float = query.astype(jnp.float32)
    keys_float = keys.astype(jnp.float32)
    clean = (segment_span == segment_before).astype(jnp.float32)
    query_decayed_rows = query_float * jnp.exp(cumulative) * clean[:, None, None]
    carried_forward = jnp.einsum(
        "ynj,njc->ync", query_decayed_rows, recurrent_state, precision=MAXIMUM_ACCURACY
    )
    order = jnp.arange(segment_span.shape[0])
    allowed = (segment_span[:, None] == segment_span[None, :]) & (order[:, None] >= order[None, :])
    gap = jnp.where(allowed[:, :, None, None], cumulative[:, None] - cumulative[None, :], 0.0)
    scores = jnp.sum(query_float[:, None] * keys_float[None, :] * jnp.exp(gap), axis=-1)
    scores = scores * allowed[:, :, None].astype(jnp.float32)
    inner = jnp.einsum(
        "tsh,shv->thv", scores.astype(jnp.bfloat16), values, preferred_element_type=jnp.float32
    )
    new_state = state_update(
        recurrent_state, cumulative, keys_float, values.astype(jnp.float32), segment_span, clean[-1]
    )
    return (new_state, (carried_forward + inner, cumulative))


def combine_states(earlier, later):
    return (earlier[0] * later[0], later[0][:, :, None] * earlier[1] + later[1])


def carry_in(decay_block, block_state):
    identity = (jnp.ones_like(decay_block), jnp.zeros_like(block_state))
    prefix = prefix_2((decay_block, block_state), "seq", combine_states, identity)
    return prefix[1]


def swiglu_rows(resident, forward_norm_scale, w_gate, w_up, down_weight):
    normed = rms_scale(resident.astype(jnp.float32), forward_norm_scale.astype(jnp.float32)).astype(
        jnp.bfloat16
    )
    every_row = lax.all_gather(normed, "req", axis=0, tiled=True)
    gate_full, up_full, down_full = (
        lax.all_gather(w_gate, "seq", axis=0, tiled=True),
        lax.all_gather(w_up, "seq", axis=0, tiled=True),
        lax.all_gather(down_weight, "seq", axis=0, tiled=True),
    )
    gate = jnp.dot(every_row, gate_full, preferred_element_type=jnp.float32)
    upward = jnp.dot(every_row, up_full, preferred_element_type=jnp.float32)
    hidden = (jax.nn.silu(gate) * upward).astype(jnp.bfloat16)
    summed = lax.psum_scatter(
        lax.dot_general(
            hidden, down_full, (((1,), (1,)), ((), ())), preferred_element_type=jnp.float32
        ),
        "req",
        scatter_dimension=0,
        tiled=True,
    )
    return summed.astype(jnp.bfloat16)


def shards(
    tokens,
    lengths,
    attn_gain,
    w_query,
    w_key,
    w_value,
    w_outgate,
    gate_down,
    gate_up,
    gate_bias,
    conv_weight,
    head_gain,
    w_out,
    forward_norm_scale,
    w_gate,
    w_up,
    down_weight,
):
    seq_count = lax.axis_size("seq")
    req_count = lax.axis_size("req")
    group_index = lax.axis_index("req")
    slice_index = lax.axis_index("seq")
    inputs = tokens[0]
    block_rows = inputs.shape[0]
    request_slots = lengths.shape[1]
    bounds_all = jnp.cumsum(lengths, axis=1)
    totals = bounds_all[:, -1]
    offsets = jnp.cumsum(totals) - totals
    group_row = jnp.arange(lengths.shape[0], dtype=jnp.int32) == group_index
    bounds = jnp.sum(jnp.where(group_row[:, None], bounds_all, 0), axis=0)
    start_pos = slice_index * block_rows
    positions = start_pos + jnp.arange(block_rows, dtype=jnp.int32)
    segment = segment_ids(positions, bounds)
    valid = segment < request_slots
    normed = rms_scale(inputs.astype(jnp.float32), attn_gain.astype(jnp.float32)).astype(
        jnp.bfloat16
    )
    projected = jnp.concatenate(
        [
            jnp.dot(normed, w_query, preferred_element_type=jnp.float32),
            jnp.dot(normed, w_key, preferred_element_type=jnp.float32),
            jnp.dot(normed, w_value, preferred_element_type=jnp.float32),
        ],
        axis=1,
    ).astype(jnp.bfloat16)
    outgate = jnp.dot(normed, w_outgate, preferred_element_type=jnp.float32)
    latent = jnp.dot(normed, gate_down, preferred_element_type=jnp.float32)
    logits = jnp.dot(latent, gate_up.astype(jnp.float32), precision=MAXIMUM_ACCURACY) + gate_bias
    log_decay = jax.nn.log_sigmoid(logits) / NORMALIZER
    taps = conv_weight.shape[0]
    edge_rows = projected[block_rows - (taps - 1) :]
    previous = from_behind(edge_rows, "seq", 1)
    extended = jnp.concatenate([previous, projected], axis=0)
    segment_ext = segment_ids(
        start_pos - (taps - 1) + jnp.arange(block_rows + taps - 1, dtype=jnp.int32), bounds
    )
    convolved = jax.nn.silu(short_conv(extended, segment_ext, conv_weight, block_rows)).astype(
        jnp.bfloat16
    )
    key_total = w_query.shape[1]
    value_total = w_value.shape[1]
    key_width = key_total // HEADS
    value_width = value_total // HEADS
    span_count = block_rows // SPAN
    query = convolved[:, :key_total].reshape(span_count, SPAN, HEADS, key_width)
    keys = convolved[:, key_total : 2 * key_total].reshape(span_count, SPAN, HEADS, key_width)
    values = convolved[:, 2 * key_total :].reshape(span_count, SPAN, HEADS, value_width)
    decay_spans = log_decay.reshape(span_count, SPAN, HEADS, key_width)
    segment_spans = segment.reshape(span_count, SPAN)
    segment_before = segment_ids(
        start_pos - 1 + SPAN * jnp.arange(span_count, dtype=jnp.int32), bounds
    )
    items = (query, keys, values, decay_spans, segment_spans, segment_before)
    block_clean = (segment[-1] == segment_before[0]).astype(jnp.float32)
    decay_block = jnp.exp(jnp.sum(log_decay, axis=0)).reshape(HEADS, key_width) * block_clean
    zero_state = jnp.zeros((HEADS, key_width, value_width), jnp.float32)
    block_state, unused = lax.scan(span_state, zero_state, items)
    incoming = carry_in(decay_block, block_state)
    final_state, (attended, cumulative) = lax.scan(span_attend, incoming, items)
    attended = attended.reshape(block_rows, HEADS, value_width)
    gated = rms_scale(attended, head_gain.astype(jnp.float32)).reshape(
        block_rows, value_total
    ) * jax.nn.silu(outgate)
    resident = (
        jnp.dot(gated.astype(jnp.bfloat16), w_out, preferred_element_type=jnp.float32)
        + inputs.astype(jnp.float32)
    ).astype(jnp.bfloat16)
    dev_count = req_count * seq_count
    own_index = group_index * seq_count + slice_index
    parallel_width = block_rows // dev_count
    capacity = 3 * block_rows // 4
    own_total = jnp.sum(jnp.where(group_row, totals, 0))
    own_offset = jnp.sum(jnp.where(group_row, offsets, 0))
    own_count = jnp.clip(own_total - start_pos, 0, block_rows)
    own_phase = (own_offset + start_pos) % dev_count
    target_slots = jnp.arange(dev_count, dtype=jnp.int32)[:, None]
    lanes = jnp.arange(parallel_width, dtype=jnp.int32)[None, :]
    source_rows = (target_slots - own_phase) % dev_count + lanes * dev_count
    outgoing = jnp.take(resident, source_rows.reshape(-1), axis=0).reshape(
        dev_count, parallel_width, -1
    )
    outgoing = jnp.where((source_rows < own_count)[:, :, None], outgoing, 0)
    arrived = lax.all_to_all(
        outgoing, ("req", "seq"), split_axis=0, concat_axis=0, tiled=True
    ).reshape(dev_count * parallel_width, -1)
    ranks = jnp.arange(capacity, dtype=jnp.int32) * dev_count + own_index
    owner = jnp.sum((ranks[:, None] >= offsets[None, :]).astype(jnp.int32), axis=1) - 1
    owner_offset = pick_group(offsets, owner)
    within = ranks - owner_offset
    owner_slice = within // block_rows
    owner_phase = (owner_offset + owner_slice * block_rows) % dev_count
    owner_lane = (owner_phase + within % block_rows) // dev_count - (
        own_index < owner_phase
    ).astype(jnp.int32)
    gathered = jnp.take(
        arrived, (owner * seq_count + owner_slice) * parallel_width + owner_lane, axis=0
    )
    processed = swiglu_rows(gathered, forward_norm_scale, w_gate, w_up, down_weight)
    senders = jnp.arange(dev_count, dtype=jnp.int32)
    sender_group = senders // seq_count
    sender_slice = senders % seq_count
    sender_base = pick_group(offsets, sender_group) + sender_slice * block_rows
    sender_phase = sender_base % dev_count
    sender_rows = (own_index - sender_phase[:, None]) % dev_count + lanes * dev_count
    sender_count = jnp.clip(
        pick_group(totals, sender_group) - sender_slice * block_rows, 0, block_rows
    )
    home_slot = jnp.clip((sender_base[:, None] + sender_rows) // dev_count, 0, capacity - 1)
    returning = jnp.take(processed, home_slot.reshape(-1), axis=0).reshape(
        dev_count, parallel_width, -1
    )
    returning = jnp.where((sender_rows < sender_count[:, None])[:, :, None], returning, 0)
    returned = lax.all_to_all(
        returning, ("req", "seq"), split_axis=0, concat_axis=0, tiled=True
    ).reshape(dev_count * parallel_width, -1)
    device_local_rows = jnp.arange(block_rows, dtype=jnp.int32)
    target_of = (own_phase + device_local_rows) % dev_count
    lane_of = (own_phase + device_local_rows) // dev_count - (target_of < own_phase).astype(
        jnp.int32
    )
    mlp_own = jnp.take(
        returned,
        jnp.clip(target_of * parallel_width + lane_of, 0, dev_count * parallel_width - 1),
        axis=0,
    )
    output = jnp.where(
        valid[:, None], resident.astype(jnp.float32) + mlp_own.astype(jnp.float32), 0.0
    ).astype(jnp.bfloat16)
    return output[None]


def solution(mesh):
    return jax.shard_map(
        shards,
        mesh=mesh,
        in_specs=(
            P("req", "seq", None),
            P(),
            P(),
            P(),
            P(),
            P(),
            P(),
            P(),
            P(),
            P(),
            P(),
            P(),
            P(),
            P(),
            P("seq", "req"),
            P("seq", "req"),
            P("seq", "req"),
        ),
        out_specs=P("req", "seq", None),
        check_vma=False,
    )
```

profile of v0, /device:TPU:1, one launch (start us, length us, event | category | flops | bytes accessed | tf_op | source)
XLA Modules:
  0.0 449.4 jit_solution(5662476398953703670)
XLA Ops:
  8.6 3.3 convolution_convert_fusion
  13.1 4.9 %collective-permute-start = (bf16[3,2048]{1,0:T(4,128)(2,1)S(1)}, bf16[3,2048]{1,0:T(4,128)(2,1)S(1)}, u32[]{:S(2)}, u32[]{:S(2)}) collective-permute-start(bf16[3,2048]{1,0:T(4,128)(2,1)S(1)} %slice.105), channel_id=1, source_target_pairs={{0,1},{1,2},{2,3},{3,4},{4,5},{5,6},{6,7},{7,8},{8,9},{9,10},{10,1... | collective-permute-start | bytes 36872 | tf_op jit(solution)/shard_map/ppermute | solution.py:33
  21.2 9.2 %while.38 = (s32[]{:T(128)}, f32[2,256,512]{2,1,0:T(8,128)S(1)}, f32[2,64,2,256]{3,2,1,0:T(2,128)S(1)}, s32[2,64]{1,0:T(2,128)S(1)}, s32[2]{0:T(128)S(1)}, /*ind...) while((s32[]{:T(128)}, f32[2,256,512]{2,1,0:T(8,128)S(1)}, ...), condition=%wide.region_8.9_spmd.clone, body=%wide.region_7.8_spmd.clone.sunk | while | flops 227418752 | bytes 3230365 | solution.py:233
  35.1 26.4 %all_gather.22 = f32[32,2,256]{2,1,0:T(2,128)S(1)} all-gather(f32[1,2,256]{2,1,0:T(2,128)S(1)} %mul.395), channel_id=1, replica_groups=mesh['req'=4,'seq'=32] {'seq'}, dimensions={0}, use_global_device_ids=true | all-gather | bytes 67584 | tf_op jit(solution)/shard_map/all_gather | solution.py:15
  62.5 84.9 %all-gather.15.cloned.1.call-done = f32[64,256,512]{2,1,0:T(8,128)} async-done(((f32[2,256,512]{2,1,0:T(8,128)}), f32[64,256,512]{2,1,0:T(8,128)}) %all-gather.15.cloned.1.call-update) | async-done | bytes 33554448 | tf_op jit(solution)/shard_map/all_gather | solution.py:15
  147.4 49.0 %while.39 = (s32[]{:T(128)}, f32[2,256,512]{2,1,0:T(8,128)S(1)}, s32[]{:T(128)}, f32[32,2,256]{2,1,0:T(2,128)S(1)}, f32[32,2,256,512]{3,2,1,0:T(8,128)}, /*index=5*/s32[]{:T(128)}, s32[]{:T(128)}) while((s32[]{:T(128)}, f32[2,256,512]{2,1,0:T(8,128)S(1)}, s32[]{:T(128)}, f32[32,2,256]{2,1,0:T(2,128)S(1)}, ...), condition=%wide.region_10.11_spmd.clone, body=%wide.region_9.10_spmd.clone.sunk | while | flops 1048580 | bytes 3151977 | solution.py:27
  156.6 1.5 fusion.165
  158.1 1.5 fusion.165
  159.7 1.5 fusion.165
  162.7 1.5 fusion.165
  164.3 1.5 fusion.165
  178.0 1.5 fusion.165
  182.7 1.5 fusion.165
  184.2 1.5 fusion.165
  188.8 1.5 fusion.165
  191.9 1.5 fusion.165
  196.5 19.7 %while.37 = (s32[]{:T(128)}, f32[2,256,512]{2,1,0:T(8,128)S(1)}, f32[2,64,2,512]{3,1,2,0:T(8,128)S(1)}, f32[2,64,2,256]{3,2,1,0:T(2,128)S(1)}, s32[2,64]{1,0:T(2...) while((s32[]{:T(128)}, f32[2,256,512]{2,1,0:T(8,128)S(1)}, ...), condition=%wide.region_13.14_spmd, body=%wide.region_11.13_spmd.sunk | while | flops 447611648 | bytes 7385501 | solution.py:235
  198.6 3.0 multiply_reduce_fusion.3
  208.4 3.0 multiply_reduce_fusion.3
  217.2 4.9 %fusion.53 = bf16[128,2048]{1,0:T(8,128)(2,1)S(1)} fusion(bf16[1024,2048]{1,0:T(8,128)(2,1)} %param.37, bf16[1,128,2048]{2,1,0:T(8,128)(2,1)S(1)} %copy-done.3, f32[128,1024]{1,0:T(8,128)S(1)} %bitcast.254, f32[128,1024]{1,0:T(8,128)S(1)} %bitcast.253, f32[1024]{0:T(1024)S(1)} %bitcast.261, bf16[2048,1024]{1,0:T(8,128)(2,1)} %param.31, ...), kind=kOutput, calls=%fused_computation.82 | convolution fusion | flops 1076625408 | bytes 10498560 | tf_op jit(solution)/shard_map/dot_general | solution.py:241
  226.0 7.1 %all-to-all-start = ((bf16[128,2,1024]{2,1,0:T(2,128)(2,1)}), bf16[128,2,1024]{2,1,0:T(2,128)(2,1)S(1)}, u32[]{:S(2)}, u32[]{:S(2)}) async-start(bf16[128,2,1024]{2,1,0:T(2,128)(2,1)} %reshape.936), calls=%async_computation | async-start | bytes 1048576 | tf_op jit(solution)/shard_map/all_to_all | solution.py:259
  233.3 13.4 %all-to-all-done = bf16[128,2,1024]{2,1,0:T(2,128)(2,1)S(1)} async-done(((bf16[128,2,1024]{2,1,0:T(2,128)(2,1)}), bf16[128,2,1024]{2,1,0:T(2,128)(2,1)S(1)}, u32[]{:S(2)}, u32[]{:S(2)}) %all-to-all-start) | async-done | bytes 524320 | tf_op jit(solution)/shard_map/all_to_all | solution.py:259
  251.3 21.3 %all-gather.7.cloned.1.call-done = bf16[384,2048]{1,0:T(8,128)(2,1)} async-done(((bf16[96,2048]{1,0:T(8,128)(2,1)}), bf16[384,2048]{1,0:T(8,128)(2,1)}) %all-gather.7.cloned.1.call-update) | async-done | bytes 1572880 | tf_op jit(solution)/shard_map/all_gather | solution.py:136
  272.6 5.2 %fusion.111 = f32[384,704]{0,1:T(8,128)} fusion(bf16[384,2048]{1,0:T(8,128)(2,1)} %all-gather.7.cloned.1.call-done, bf16[2048,704]{1,0:T(8,128)(2,1)} %all-gather.9.cloned.1.call-done), kind=kOutput, calls=%fused_computation.264 | convolution fusion | flops 1107296256 | bytes 5537792 | tf_op jit(solution)/shard_map/dot_general | solution.py:142
  277.7 42.4 %all-gather.11.cloned.1.call-done = bf16[2048,704]{1,0:T(8,128)(2,1)} async-done(((bf16[64,704]{1,0:T(8,128)(2,1)}), bf16[2048,704]{1,0:T(8,128)(2,1)}) %all-gather.11.cloned.1.call-update) | async-done | bytes 2883600 | tf_op jit(solution)/shard_map/all_gather | solution.py:139
  320.2 46.3 %all-gather.13.cloned.1.call-done = bf16[2048,704]{1,0:T(8,128)(2,1)} async-done(((bf16[64,704]{1,0:T(8,128)(2,1)}), bf16[2048,704]{1,0:T(8,128)(2,1)}) %all-gather.13.cloned.1.call-update) | async-done | bytes 2883600 | tf_op jit(solution)/shard_map/all_gather | solution.py:140
  366.5 7.9 %fusion.62 = f32[384,2048]{1,0:T(8,128)} fusion(bf16[2048,704]{1,0:T(8,128)(2,1)} %all-gather.13.cloned.1.call-done, bf16[384,2048]{1,0:T(8,128)(2,1)S(1)} %copy-done.9, bf16[2048,704]{1,0:T(8,128)(2,1)} %all-gather.11.cloned.1.call-done, f32[384,704]{0,1:T(8,128)} %fusion.111), kind=kOutput, calls=%fused_computation.103 | convolution fusion | flops 2216214528 | bytes 11567104 | tf_op jit(solution)/shard_map/dot_general | solution.py:146
  374.7 37.1 %reduce-scatter.2.cloned.1.call-done = f32[96,2048]{1,0:T(8,128)} async-done(((f32[384,2048]{1,0:T(8,128)}), f32[96,2048]{1,0:T(8,128)}) %reduce-scatter.2.cloned.1.call-update) | async-done | bytes 786448 | tf_op jit(solution)/shard_map/reduce_scatter | solution.py:145
  416.2 8.0 %all-to-all-start.1 = ((bf16[128,2,1024]{2,1,0:T(2,128)(2,1)}), bf16[128,2,1024]{2,1,0:T(2,128)(2,1)S(1)}, u32[]{:S(2)}, u32[]{:S(2)}) async-start(bf16[128,2,1024]{2,1,0:T(2,128)(2,1)} %reshape.938), calls=%async_computation.2 | async-start | bytes 1048576 | tf_op jit(solution)/shard_map/all_to_all | solution.py:289
  424.3 13.5 %all-to-all-done.1 = bf16[128,2,1024]{2,1,0:T(2,128)(2,1)S(1)} async-done(((bf16[128,2,1024]{2,1,0:T(2,128)(2,1)}), bf16[128,2,1024]{2,1,0:T(2,128)(2,1)S(1)}, u32[]{:S(2)}, u32[]{:S(2)}) %all-to-all-start.1) | async-done | bytes 524320 | tf_op jit(solution)/shard_map/all_to_all | solution.py:289
  438.6 1.7 gather_fusion.3
  440.3 2.2 fusion.64
  (247 shorter events, 77.6 us)
Async XLA Ops:
  6.5 5.4 %copy-start = (bf16[2048,512]{1,0:T(8,128)(2,1)S(1)}, bf16[2048,512]{1,0:T(8,128)(2,1)}, u32[]{:S(2)}) copy-start(bf16[2048,512]{1,0:T(8,128)(2,1)} %param.29) | copy-start | bytes 6291460
  6.5 5.4 %copy-start.3 = (bf16[1,128,2048]{2,1,0:T(8,128)(2,1)S(1)}, bf16[1,128,2048]{2,1,0:T(8,128)(2,1)}, u32[]{:S(2)}) copy-start(bf16[1,128,2048]{2,1,0:T(8,128)(2,1)} %param.25) | copy-start | bytes 1572868
  6.5 140.9 %all-gather.15.cloned.1.call-start = ((), (), s32[]{:S(2)}) async-start(), calls=%async_computation.8 | async-start | bytes 34603008 | tf_op jit(solution)/shard_map/all_gather | solution.py:15
  8.6 3.8 copy-start.8
  11.9 6.1 %copy-start.6 = (s32[4,4]{1,0:T(4,128)S(1)}, s32[4,4]{1,0:T(4,128)}, u32[]{:S(2)}) copy-start(s32[4,4]{1,0:T(4,128)} %param.26) | copy-start | bytes 196
  11.9 6.6 %copy-start.4 = (bf16[4,2048]{1,0:T(4,128)(2,1)S(1)}, bf16[4,2048]{1,0:T(4,128)(2,1)}, u32[]{:S(2)}) copy-start(bf16[4,2048]{1,0:T(4,128)(2,1)} %param.35) | copy-start | bytes 49156
  11.9 6.7 %copy-start.10 = (bf16[2048,16]{0,1:T(8,128)(2,1)S(1)}, bf16[2048,16]{0,1:T(8,128)(2,1)}, u32[]{:S(2)}) copy-start(bf16[2048,16]{0,1:T(8,128)(2,1)} %param.32) | copy-start | bytes 196612
  12.5 6.5 %copy-start.11 = (bf16[16,512]{1,0:T(8,128)(2,1)S(1)}, bf16[16,512]{1,0:T(8,128)(2,1)}, u32[]{:S(2)}) copy-start(bf16[16,512]{1,0:T(8,128)(2,1)} %param.33) | copy-start | bytes 49156
  12.5 6.5 %copy-start.12 = (f32[512]{0:T(512)S(1)}, f32[512]{0:T(512)}, u32[]{:S(2)}) copy-start(f32[512]{0:T(512)} %param.34) | copy-start | bytes 6148
  13.1 6.8 %collective-permute-start = (bf16[3,2048]{1,0:T(4,128)(2,1)S(1)}, bf16[3,2048]{1,0:T(4,128)(2,1)S(1)}, u32[]{:S(2)}, u32[]{:S(2)}) collective-permute-start(bf16[3,2048]{1,0:T(4,128)(2,1)S(1)} %slice.105), channel_id=1, source_target_pairs={{0,1},{1,2},{2,3},{3,4},{4,5},{5,6},{6,7},{7,8},{8,9},{9,10},{10,1... | collective-permute-start | bytes 36872 | tf_op jit(solution)/shard_map/ppermute | solution.py:33
  21.2 40.4 %copy-start.7 = (bf16[512]{0:T(512)(128)(2,1)S(1)}, bf16[512]{0:T(512)(128)(2,1)}, u32[]{:S(2)}) copy-start(bf16[512]{0:T(512)(128)(2,1)} %param.36) | copy-start | bytes 3076
  21.2 41.3 %copy-start.5 = (bf16[2048]{0:T(1024)(128)(2,1)S(1)}, bf16[2048]{0:T(1024)(128)(2,1)}, u32[]{:S(2)}) copy-start(bf16[2048]{0:T(1024)(128)(2,1)} %param.38) | copy-start | bytes 12292
  30.4 1.0 copy-start.2
  31.5 219.8 %all-gather.9.cloned.1.call-start = ((), (), s32[]{:S(2)}) async-start(), calls=%async_computation.4 | async-start | bytes 3244032 | tf_op jit(solution)/shard_map/all_gather | solution.py:138
  226.0 20.7 %all-to-all-start = ((bf16[128,2,1024]{2,1,0:T(2,128)(2,1)}), bf16[128,2,1024]{2,1,0:T(2,128)(2,1)S(1)}, u32[]{:S(2)}, u32[]{:S(2)}) async-start(bf16[128,2,1024]{2,1,0:T(2,128)(2,1)} %reshape.936), calls=%async_computation | async-start | bytes 1048576 | tf_op jit(solution)/shard_map/all_to_all | solution.py:259
  233.2 39.4 %all-gather.7.cloned.1.call-start = ((), (), s32[]{:S(2)}) async-start(), calls=%async_computation.3 | async-start | bytes 1966080 | tf_op jit(solution)/shard_map/all_gather | solution.py:136
  249.8 70.3 %all-gather.11.cloned.1.call-start = ((), (), s32[]{:S(2)}) async-start(), calls=%async_computation.5 | async-start | bytes 3244032 | tf_op jit(solution)/shard_map/all_gather | solution.py:139
  250.4 116.1 %all-gather.13.cloned.1.call-start = ((), (), s32[]{:S(2)}) async-start(), calls=%async_computation.6 | async-start | bytes 3244032 | tf_op jit(solution)/shard_map/all_gather | solution.py:140
  251.0 160.7 %reduce-scatter.2.cloned.1.call-start = ((), (), s32[]{:S(2)}) async-start(), calls=%async_computation.7 | async-start | bytes 3932160 | tf_op jit(solution)/shard_map/reduce_scatter | solution.py:145
  272.6 93.9 %copy-start.9 = (bf16[384,2048]{1,0:T(8,128)(2,1)S(1)}, bf16[384,2048]{1,0:T(8,128)(2,1)}, u32[]{:S(2)}) copy-start(bf16[384,2048]{1,0:T(8,128)(2,1)} %all-gather.7.cloned.1.call-done) | copy-start | bytes 4718596
  416.2 21.6 %all-to-all-start.1 = ((bf16[128,2,1024]{2,1,0:T(2,128)(2,1)}), bf16[128,2,1024]{2,1,0:T(2,128)(2,1)S(1)}, u32[]{:S(2)}, u32[]{:S(2)}) async-start(bf16[128,2,1024]{2,1,0:T(2,128)(2,1)} %reshape.938), calls=%async_computation.2 | async-start | bytes 1048576 | tf_op jit(solution)/shard_map/all_to_all | solution.py:289
  438.6 4.0 copy-start.1
Sparse Core Ops, SparseCore 0:
  31.6 115.7 all-gather.14
  149.7 44.1 all-gather.8
  250.0 22.5 all-gather.6
  274.7 45.4 all-gather.10
  322.3 44.2 all-gather.12
  374.6 37.1 reduce-scatter.1
where the time goes:
time: 451 us; the launch traced here: 449 us
  waiting for transfers between devices  261 us (58%)
  other arithmetic  71.9 us (16%)
  matrix products  29.9 us (7%)
  blocking collectives  26.4 us (6%)
  starting transfers between devices  20.5 us (5%)
  local copies, waits for them, and re-layouts  19.7 us (4%)
  between operations  15.9 us (4%)
    all_gather x1, waiting for transfers between devices, prefix_2(): everything = jax.tree.map(lambda part: lax.all_gather(part, axis), shard)  84.9 us
    select_n x32, other arithmetic, lap(): return jax.tree.map(lambda a, b: jnp.where(reached, a, b), new, before)  47.7 us
    all_gather x1, waiting for transfers between devices, swiglu_rows(): lax.all_gather(down_weight, 'seq', axis=0, tiled=True)  46.3 us
    all_gather x1, waiting for transfers between devices, swiglu_rows(): lax.all_gather(w_up, 'seq', axis=0, tiled=True)  42.4 us
    reduce_scatter x1, waiting for transfers between devices, swiglu_rows(): lax.psum_scatter(lax.dot_general(hidden, down_full, (((1,), (1,)), ((), (...  37.1 us
    all_gather x1, blocking collectives, prefix_2(): everything = jax.tree.map(lambda part: lax.all_gather(part, axis), shard)  26.4 us
    all_gather x1, waiting for transfers between devices, swiglu_rows(): every_row = lax.all_gather(normed, 'req', axis=0, tiled=True)  21.3 us
    all_to_all x1, waiting for transfers between devices, shards(): lax.all_to_all(returning, ('req', 'seq'), split_axis=0, concat_axis=0, ti...  13.5 us
  transfers between devices with their start and end apart: 9, of which 7 were waited for; matrix products, arithmetic and copies ran while one was open for 20% of the time, Pallas kernels for 0%

commit v1 on v0

--- a/solution.py
+++ b/solution.py
@@ -133,7 +133,21 @@
     normed = rms_scale(resident.astype(jnp.float32), forward_norm_scale.astype(jnp.float32)).astype(
         jnp.bfloat16
     )
-    every_row = lax.all_gather(normed, "req", axis=0, tiled=True)
+    ways, here, step = (lax.axis_size("req"), lax.axis_index("req"), normed.shape[0])
+    lengths_2 = [n * ways if d == 0 else n for d, n in enumerate(normed.shape)]
+    full = lax.dynamic_update_slice_in_dim(
+        jnp.zeros(lengths_2, normed.dtype), normed, here * step, axis=0
+    )
+    going_up = going_down = normed
+    for far in range(1, ways // 2 + 1):
+        going_up = lax.ppermute(going_up, "req", [(d, (d + 1) % ways) for d in range(ways)])
+        full = lax.dynamic_update_slice_in_dim(full, going_up, (here - far) % ways * step, axis=0)
+        if 2 * far < ways:
+            going_down = lax.ppermute(going_down, "req", [(d, (d - 1) % ways) for d in range(ways)])
+            full = lax.dynamic_update_slice_in_dim(
+                full, going_down, (here + far) % ways * step, axis=0
+            )
+    every_row = full
     gate_full, up_full, down_full = (
         lax.all_gather(w_gate, "seq", axis=0, tiled=True),
         lax.all_gather(w_up, "seq", axis=0, tiled=True),

time: 451 us -> 376 us (0.83)
  waiting for transfers between devices: 261 us -> 184 us
    all_gather x1, waiting for transfers between devices: 46.3 us -> 0.01 us  [swiglu_rows(): lax.all_gather(down_weight, 'seq', axis=0, tiled=True)]
    all_gather x1, waiting for transfers between devices: 42.4 us -> 15 us  [swiglu_rows(): lax.all_gather(w_up, 'seq', axis=0, tiled=True)]
    all_gather x1 -> x0, waiting for transfers between devices: 21.3 us -> none  [swiglu_rows(): every_row = lax.all_gather(normed, 'req', axis=0, tiled=True)]
    ppermute x0 -> x3, waiting for transfers between devices: none -> 18.2 us  [the longest x2 18.2 us: swiglu_rows(): lax.ppermute(going_up, 'req', [(d, (d + 1) % ways) for d in range(ways)])]
  transfers between devices with their start and end apart: 9 -> 11, of which waited for: 7 -> 7; matrix products, arithmetic and copies ran while one was open for 20% -> 24% of each run, Pallas kernels for 0% -> 0%
where the time goes in v1:
time: 376 us; the launch traced here: 374 us
  waiting for transfers between devices  184 us (49%)
  other arithmetic  71.2 us (19%)
  matrix products  29.2 us (8%)
  blocking collectives  26.4 us (7%)
  starting transfers between devices  23 us (6%)
  local copies, waits for them, and re-layouts  21.1 us (6%)
  between operations  15.6 us (4%)
  loops' own time  4.02 us (1%)
    all_gather x1, waiting for transfers between devices, prefix_2(): everything = jax.tree.map(lambda part: lax.all_gather(part, axis), shard)  83.6 us
    select_n x32, other arithmetic, lap(): return jax.tree.map(lambda a, b: jnp.where(reached, a, b), new, before)  47.7 us
    reduce_scatter x1, waiting for transfers between devices, swiglu_rows(): lax.psum_scatter(lax.dot_general(hidden, down_full, (((1,), (1,)), ((), (...  37.1 us
    all_gather x1, blocking collectives, prefix_2(): everything = jax.tree.map(lambda part: lax.all_gather(part, axis), shard)  26.4 us
    ppermute x2, waiting for transfers between devices, swiglu_rows(): lax.ppermute(going_up, 'req', [(d, (d + 1) % ways) for d in range(ways)])  18.2 us
    all_gather x1, waiting for transfers between devices, swiglu_rows(): lax.all_gather(w_up, 'seq', axis=0, tiled=True)  15 us
    all_to_all x1, waiting for transfers between devices, shards(): lax.all_to_all(outgoing, ('req', 'seq'), split_axis=0, concat_axis=0, til...  14.5 us
    all_to_all x1, waiting for transfers between devices, shards(): lax.all_to_all(returning, ('req', 'seq'), split_axis=0, concat_axis=0, ti...  13.5 us
  transfers between devices with their start and end apart: 11, of which 7 were waited for; matrix products, arithmetic and copies ran while one was open for 24% of the time, Pallas kernels for 0%

profile of v1, /device:TPU:1, one launch (start us, length us, event | category | flops | bytes accessed | tf_op | source)
XLA Modules:
  0.0 374.3 jit_solution(17466149721229861402)
XLA Ops:
  8.6 3.2 convolution_convert_fusion
  14.0 4.9 %collective-permute-start = (bf16[3,2048]{1,0:T(4,128)(2,1)S(1)}, bf16[3,2048]{1,0:T(4,128)(2,1)S(1)}, u32[]{:S(2)}, u32[]{:S(2)}) collective-permute-start(bf16[3,2048]{1,0:T(4,128)(2,1)S(1)} %slice.105), channel_id=1, source_target_pairs={{0,1},{1,2},{2,3},{3,4},{4,5},{5,6},{6,7},{7,8},{8,9},{9,10},{10,1... | collective-permute-start | bytes 36872 | tf_op jit(solution)/shard_map/ppermute | solution.py:33
  22.1 9.0 %while.38 = (s32[]{:T(128)}, f32[2,256,512]{2,1,0:T(8,128)S(1)}, f32[2,64,2,256]{3,2,1,0:T(2,128)S(1)}, s32[2,64]{1,0:T(2,128)S(1)}, s32[2]{0:T(128)S(1)}, /*ind...) while((s32[]{:T(128)}, f32[2,256,512]{2,1,0:T(8,128)S(1)}, ...), condition=%wide.region_8.9_spmd.clone, body=%wide.region_7.8_spmd.clone.sunk | while | flops 227418752 | bytes 3230365 | solution.py:247
  37.2 26.4 %all_gather.19 = f32[32,2,256]{2,1,0:T(2,128)S(1)} all-gather(f32[1,2,256]{2,1,0:T(2,128)S(1)} %mul.407), channel_id=1, replica_groups=mesh['req'=4,'seq'=32] {'seq'}, dimensions={0}, use_global_device_ids=true | all-gather | bytes 67584 | tf_op jit(solution)/shard_map/all_gather | solution.py:15
  64.5 83.6 %all-gather.12.cloned.1.call-done = f32[64,256,512]{2,1,0:T(8,128)} async-done(((f32[2,256,512]{2,1,0:T(8,128)}), f32[64,256,512]{2,1,0:T(8,128)}) %all-gather.12.cloned.1.call-update) | async-done | bytes 33554448 | tf_op jit(solution)/shard_map/all_gather | solution.py:15
  148.2 49.0 %while.39 = (s32[]{:T(128)}, f32[2,256,512]{2,1,0:T(8,128)S(1)}, s32[]{:T(128)}, f32[32,2,256]{2,1,0:T(2,128)S(1)}, f32[32,2,256,512]{3,2,1,0:T(8,128)}, /*index=5*/s32[]{:T(128)}, s32[]{:T(128)}) while((s32[]{:T(128)}, f32[2,256,512]{2,1,0:T(8,128)S(1)}, s32[]{:T(128)}, f32[32,2,256]{2,1,0:T(2,128)S(1)}, ...), condition=%wide.region_10.11_spmd.clone, body=%wide.region_9.10_spmd.clone.sunk | while | flops 1048580 | bytes 3151977 | solution.py:27
  158.9 1.5 fusion.167
  160.4 1.5 fusion.167
  163.5 1.5 fusion.167
  165.0 1.5 fusion.167
  178.7 1.5 fusion.167
  183.4 1.5 fusion.167
  184.9 1.5 fusion.167
  189.6 1.5 fusion.167
  192.6 1.5 fusion.167
  197.2 19.7 %while.37 = (s32[]{:T(128)}, f32[2,256,512]{2,1,0:T(8,128)S(1)}, f32[2,64,2,512]{3,1,2,0:T(8,128)S(1)}, f32[2,64,2,256]{3,2,1,0:T(2,128)S(1)}, s32[2,64]{1,0:T(2...) while((s32[]{:T(128)}, f32[2,256,512]{2,1,0:T(8,128)S(1)}, ...), condition=%wide.region_13.14_spmd, body=%wide.region_11.13_spmd.sunk | while | flops 447611648 | bytes 7385501 | solution.py:249
  199.3 3.0 multiply_reduce_fusion.3
  209.2 3.0 multiply_reduce_fusion.3
  218.0 4.9 %fusion.53 = bf16[128,2048]{1,0:T(8,128)(2,1)S(1)} fusion(bf16[1024,2048]{1,0:T(8,128)(2,1)} %param.37, bf16[1,128,2048]{2,1,0:T(8,128)(2,1)S(1)} %copy-done.3, f32[128,1024]{1,0:T(8,128)S(1)} %bitcast.254, f32[128,1024]{1,0:T(8,128)S(1)} %bitcast.253, f32[1024]{0:T(1024)S(1)} %bitcast.261, bf16[2048,1024]{1,0:T(8,128)(2,1)} %param.31, ...), kind=kOutput, calls=%fused_computation.82 | convolution fusion | flops 1076625408 | bytes 10498560 | tf_op jit(solution)/shard_map/dot_general | solution.py:255
  226.8 7.1 %all-to-all-start = ((bf16[128,2,1024]{2,1,0:T(2,128)(2,1)}), bf16[128,2,1024]{2,1,0:T(2,128)(2,1)S(1)}, u32[]{:S(2)}, u32[]{:S(2)}) async-start(bf16[128,2,1024]{2,1,0:T(2,128)(2,1)} %reshape.936), calls=%async_computation | async-start | bytes 1048576 | tf_op jit(solution)/shard_map/all_to_all | solution.py:273
  234.1 14.5 %all-to-all-done = bf16[128,2,1024]{2,1,0:T(2,128)(2,1)S(1)} async-done(((bf16[128,2,1024]{2,1,0:T(2,128)(2,1)}), bf16[128,2,1024]{2,1,0:T(2,128)(2,1)S(1)}, u32[]{:S(2)}, u32[]{:S(2)}) %all-to-all-start) | async-done | bytes 524320 | tf_op jit(solution)/shard_map/all_to_all | solution.py:273
  251.5 2.4 collective-permute-start.2
  253.8 8.2 %collective-permute-done.1 = bf16[96,2048]{1,0:T(8,128)(2,1)S(1)} collective-permute-done((bf16[96,2048]{1,0:T(8,128)(2,1)S(1)}, bf16[96,2048]{1,0:T(8,128)(2,1)S(1)}, u32[]{:S(2)}, u32[]{:S(2)}) %collective-permute-start.1) | collective-permute-done | bytes 393248 | tf_op jit(solution)/shard_map/ppermute | solution.py:143
  262.2 10.0 %collective-permute-done.3 = bf16[96,2048]{1,0:T(8,128)(2,1)S(1)} collective-permute-done((bf16[96,2048]{1,0:T(8,128)(2,1)S(1)}, bf16[96,2048]{1,0:T(8,128)(2,1)S(1)}, u32[]{:S(2)}, u32[]{:S(2)}) %collective-permute-start.3) | collective-permute-done | bytes 393248 | tf_op jit(solution)/shard_map/ppermute | solution.py:143
  272.2 4.6 %fusion.113 = f32[384,704]{0,1:T(8,128)} fusion(bf16[384,2048]{1,0:T(8,128)(2,1)S(1)} %constant_dynamic-update-slice_fusion, bf16[2048,704]{1,0:T(8,128)(2,1)} %all-gather.6.cloned.1.call-done), kind=kOutput, calls=%fused_computation.268 | convolution fusion | flops 1107296256 | bytes 5537792 | tf_op jit(solution)/shard_map/dot_general | solution.py:156
  276.8 15.0 %all-gather.8.cloned.1.call-done = bf16[2048,704]{1,0:T(8,128)(2,1)} async-done(((bf16[64,704]{1,0:T(8,128)(2,1)}), bf16[2048,704]{1,0:T(8,128)(2,1)}) %all-gather.8.cloned.1.call-update) | async-done | bytes 2883600 | tf_op jit(solution)/shard_map/all_gather | solution.py:153
  291.8 7.9 %fusion.61 = f32[384,2048]{1,0:T(8,128)} fusion(bf16[2048,704]{1,0:T(8,128)(2,1)} %all-gather.10.cloned.1.call-done, f32[384,704]{0,1:T(8,128)} %fusion.113, bf16[384,2048]{1,0:T(8,128)(2,1)S(1)} %constant_dynamic-update-slice_fusion, bf16[2048,704]{1,0:T(8,128)(2,1)} %all-gather.8.cloned.1.call-done), kind=kOutput, calls=%fused_computation.103 | convolution fusion | flops 2216214528 | bytes 11567104 | tf_op jit(solution)/shard_map/dot_general | solution.py:160
  299.9 37.1 %reduce-scatter.2.cloned.1.call-done = f32[96,2048]{1,0:T(8,128)} async-done(((f32[384,2048]{1,0:T(8,128)}), f32[96,2048]{1,0:T(8,128)}) %reduce-scatter.2.cloned.1.call-update) | async-done | bytes 786448 | tf_op jit(solution)/shard_map/reduce_scatter | solution.py:159
  341.5 8.0 %all-to-all-start.1 = ((bf16[128,2,1024]{2,1,0:T(2,128)(2,1)}), bf16[128,2,1024]{2,1,0:T(2,128)(2,1)S(1)}, u32[]{:S(2)}, u32[]{:S(2)}) async-start(bf16[128,2,1024]{2,1,0:T(2,128)(2,1)} %reshape.938), calls=%async_computation.2 | async-start | bytes 1048576 | tf_op jit(solution)/shard_map/all_to_all | solution.py:303
  349.6 13.5 %all-to-all-done.1 = bf16[128,2,1024]{2,1,0:T(2,128)(2,1)S(1)} async-done(((bf16[128,2,1024]{2,1,0:T(2,128)(2,1)}), bf16[128,2,1024]{2,1,0:T(2,128)(2,1)S(1)}, u32[]{:S(2)}, u32[]{:S(2)}) %all-to-all-start.1) | async-done | bytes 524320 | tf_op jit(solution)/shard_map/all_to_all | solution.py:303
  363.8 1.7 gather_fusion.3
  365.6 2.2 fusion.63
  (251 shorter events, 80.0 us)
Async XLA Ops:
  6.5 5.3 %copy-start = (bf16[2048,512]{1,0:T(8,128)(2,1)S(1)}, bf16[2048,512]{1,0:T(8,128)(2,1)}, u32[]{:S(2)}) copy-start(bf16[2048,512]{1,0:T(8,128)(2,1)} %param.29) | copy-start | bytes 6291460
  6.5 141.6 %all-gather.12.cloned.1.call-start = ((), (), s32[]{:S(2)}) async-start(), calls=%async_computation.7 | async-start | bytes 34603008 | tf_op jit(solution)/shard_map/all_gather | solution.py:15
  8.6 3.2 copy-start.3
  11.8 1.6 copy-start.8
  13.4 5.6 %copy-start.6 = (s32[4,4]{1,0:T(4,128)S(1)}, s32[4,4]{1,0:T(4,128)}, u32[]{:S(2)}) copy-start(s32[4,4]{1,0:T(4,128)} %param.26) | copy-start | bytes 196
  13.4 6.0 %copy-start.4 = (bf16[4,2048]{1,0:T(4,128)(2,1)S(1)}, bf16[4,2048]{1,0:T(4,128)(2,1)}, u32[]{:S(2)}) copy-start(bf16[4,2048]{1,0:T(4,128)(2,1)} %param.35) | copy-start | bytes 49156
  13.4 6.1 %copy-start.9 = (bf16[2048,16]{0,1:T(8,128)(2,1)S(1)}, bf16[2048,16]{0,1:T(8,128)(2,1)}, u32[]{:S(2)}) copy-start(bf16[2048,16]{0,1:T(8,128)(2,1)} %param.32) | copy-start | bytes 196612
  13.4 6.4 %copy-start.10 = (bf16[16,512]{1,0:T(8,128)(2,1)S(1)}, bf16[16,512]{1,0:T(8,128)(2,1)}, u32[]{:S(2)}) copy-start(bf16[16,512]{1,0:T(8,128)(2,1)} %param.33) | copy-start | bytes 49156
  13.4 6.4 %copy-start.11 = (f32[512]{0:T(512)S(1)}, f32[512]{0:T(512)}, u32[]{:S(2)}) copy-start(f32[512]{0:T(512)} %param.34) | copy-start | bytes 6148
  14.0 6.8 %collective-permute-start = (bf16[3,2048]{1,0:T(4,128)(2,1)S(1)}, bf16[3,2048]{1,0:T(4,128)(2,1)S(1)}, u32[]{:S(2)}, u32[]{:S(2)}) collective-permute-start(bf16[3,2048]{1,0:T(4,128)(2,1)S(1)} %slice.105), channel_id=1, source_target_pairs={{0,1},{1,2},{2,3},{3,4},{4,5},{5,6},{6,7},{7,8},{8,9},{9,10},{10,1... | collective-permute-start | bytes 36872 | tf_op jit(solution)/shard_map/ppermute | solution.py:33
  22.1 41.6 %copy-start.7 = (bf16[512]{0:T(512)(128)(2,1)S(1)}, bf16[512]{0:T(512)(128)(2,1)}, u32[]{:S(2)}) copy-start(bf16[512]{0:T(512)(128)(2,1)} %param.36) | copy-start | bytes 3076
  22.1 42.4 %copy-start.5 = (bf16[2048]{0:T(1024)(128)(2,1)S(1)}, bf16[2048]{0:T(1024)(128)(2,1)}, u32[]{:S(2)}) copy-start(bf16[2048]{0:T(1024)(128)(2,1)} %param.38) | copy-start | bytes 12292
  31.2 1.0 copy-start.2
  32.2 240.0 %all-gather.6.cloned.1.call-start = ((), (), s32[]{:S(2)}) async-start(), calls=%async_computation.3 | async-start | bytes 3244032 | tf_op jit(solution)/shard_map/all_gather | solution.py:152
  33.0 243.8 %all-gather.10.cloned.1.call-start = ((), (), s32[]{:S(2)}) async-start(), calls=%async_computation.5 | async-start | bytes 3244032 | tf_op jit(solution)/shard_map/all_gather | solution.py:154
  33.7 258.1 %all-gather.8.cloned.1.call-start = ((), (), s32[]{:S(2)}) async-start(), calls=%async_computation.4 | async-start | bytes 3244032 | tf_op jit(solution)/shard_map/all_gather | solution.py:153
  226.8 21.7 %all-to-all-start = ((bf16[128,2,1024]{2,1,0:T(2,128)(2,1)}), bf16[128,2,1024]{2,1,0:T(2,128)(2,1)S(1)}, u32[]{:S(2)}, u32[]{:S(2)}) async-start(bf16[128,2,1024]{2,1,0:T(2,128)(2,1)} %reshape.936), calls=%async_computation | async-start | bytes 1048576 | tf_op jit(solution)/shard_map/all_to_all | solution.py:273
  233.9 103.1 %reduce-scatter.2.cloned.1.call-start = ((), (), s32[]{:S(2)}) async-start(), calls=%async_computation.6 | async-start | bytes 3932160 | tf_op jit(solution)/shard_map/reduce_scatter | solution.py:159
  251.1 11.0 %collective-permute-start.1 = (bf16[96,2048]{1,0:T(8,128)(2,1)S(1)}, bf16[96,2048]{1,0:T(8,128)(2,1)S(1)}, u32[]{:S(2)}, u32[]{:S(2)}) collective-permute-start(bf16[96,2048]{1,0:T(8,128)(2,1)S(1)} %get-tuple-element.358), channel_id=1, source_target_pairs={{0,32},{32,64},{64,96},{96,0},{1,33},{33,65},{65,97},{97,1},{2,34}... | collective-permute-start | bytes 1179656 | tf_op jit(solution)/shard_map/ppermute | solution.py:143
  251.5 10.7 %collective-permute-start.2 = (bf16[96,2048]{1,0:T(8,128)(2,1)S(1)}, bf16[96,2048]{1,0:T(8,128)(2,1)S(1)}, u32[]{:S(2)}, u32[]{:S(2)}) collective-permute-start(bf16[96,2048]{1,0:T(8,128)(2,1)S(1)} %get-tuple-element.358), channel_id=1, source_target_pairs={{0,96},{32,0},{64,32},{96,64},{1,97},{33,1},{65,33},{97,65},{2,98}... | collective-permute-start | bytes 1179656 | tf_op jit(solution)/shard_map/ppermute | solution.py:146
  262.1 10.1 %collective-permute-start.3 = (bf16[96,2048]{1,0:T(8,128)(2,1)S(1)}, bf16[96,2048]{1,0:T(8,128)(2,1)S(1)}, u32[]{:S(2)}, u32[]{:S(2)}) collective-permute-start(bf16[96,2048]{1,0:T(8,128)(2,1)S(1)} %collective-permute-done.1), channel_id=1, source_target_pairs={{0,32},{32,64},{64,96},{96,0},{1,33},{33,65},{65,97},{97,1},{2,34}... | collective-permute-start | bytes 1179656 | tf_op jit(solution)/shard_map/ppermute | solution.py:143
  341.5 21.6 %all-to-all-start.1 = ((bf16[128,2,1024]{2,1,0:T(2,128)(2,1)}), bf16[128,2,1024]{2,1,0:T(2,128)(2,1)S(1)}, u32[]{:S(2)}, u32[]{:S(2)}) async-start(bf16[128,2,1024]{2,1,0:T(2,128)(2,1)} %reshape.938), calls=%async_computation.2 | async-start | bytes 1048576 | tf_op jit(solution)/shard_map/all_to_all | solution.py:303
  363.8 4.0 %copy-start.1 = (bf16[2048,512]{1,0:T(8,128)(2,1)S(1)}, bf16[2048,512]{1,0:T(8,128)(2,1)}, u32[]{:S(2)}) copy-start(bf16[2048,512]{1,0:T(8,128)(2,1)} %param.29) | copy-start | bytes 6291460
Sparse Core Ops, SparseCore 0:
  32.3 115.7 all-gather.11
  150.4 44.1 all-gather.5
  196.8 47.6 all-gather.9
  246.7 45.0 all-gather.7
  299.8 37.1 reduce-scatter.1
